TPU v7x, 32 devices: a whole 2x2x4 slice. The times are simulated.
32 devices in a mesh: batch: 2 (over x), ctx: 4 (over y, core), mp: 4 (over z).
Axes of the slice: x: 2, y: 2, z: 4, core: 2. Of those that a mesh axis runs over, the one named last changes fastest.
Arguments:
- hidden_in: bfloat16 [4, 512, 1024], P('batch', 'ctx'), may hold values from -6 to 6
- segment_ids: int32 [4, 512], P('batch', 'ctx'), may hold values from 0 to 3, never falling along the last dimension, each value on 1 to 256 neighbouring positions
- gains: bfloat16 [2, 2, 1024], P(None, None, ('batch', 'ctx', 'mp')), may hold values from 0.5 to 1.5
- biases: bfloat16 [2, 10, 1024], P(None, None, ('batch', 'ctx', 'mp')), may hold values from -3 to 3
- w_qkv: bfloat16 [2, 1024, 3, 1024], P(None, ('batch', 'ctx'), None, 'mp'), may hold values from -0.1875 to 0.1875
- w_out_t: bfloat16 [2, 1024, 1024], P(None, ('batch', 'ctx'), 'mp'), may hold values from -0.5 to 0.5
- w_up: bfloat16 [2, 1024, 4096], P(None, ('batch', 'ctx'), 'mp'), may hold values from -0.1875 to 0.1875
- w_down_t: bfloat16 [2, 1024, 4096], P(None, ('batch', 'ctx'), 'mp'), may hold values from -0.09375 to 0.09375
- grad_out: bfloat16 [4, 512, 1024], P('batch', 'ctx'), may hold values from -6 to 6
Outputs:
- output: bfloat16 [4, 512, 1024], P('batch', 'ctx')
- grad_in: bfloat16 [4, 512, 1024], P('batch', 'ctx')
- grad_gains: float32 [2, 2, 1024], P(None, None, ('batch', 'ctx', 'mp'))
- grad_biases: float32 [2, 10, 1024], P(None, None, ('batch', 'ctx', 'mp'))
- grad_qkv: float32 [2, 1024, 3, 1024], P(None, ('batch', 'ctx'), None, 'mp')
- grad_attn_out: float32 [2, 1024, 1024], P(None, ('batch', 'ctx'), 'mp')
- grad_up: float32 [2, 1024, 4096], P(None, ('batch', 'ctx'), 'mp')
- grad_down: float32 [2, 1024, 4096], P(None, ('batch', 'ctx'), 'mp')
Inputs may be any that keep to these rules, and one draw needn't show every extreme that they name: `segment_ids`: document numbers never fall along a sequence; every document spans 1 to 256 tokens, and one of each sequence spans exactly that many.
All inputs are finite; a program needn't handle non-finite values.
Results may differ from a plain program's by a relative error of at most 0.023.
Values may be sent and summed in bfloat16 or wider, within the bound.
A program may use at most 128 MiB of HBM per device.

v0:
```python
import math
import jax
import jax.numpy as jnp
from jax import lax
from jax.sharding import PartitionSpec as P

HEADS = 16
HEAD = 64
EPS = 1e-05
GELU_C = 0.7978845608028654
GELU_K = 0.044715


def norm_parts(values):
    center = values - jnp.mean(values, -1, keepdims=True)
    inverse = lax.rsqrt(jnp.mean(center * center, -1, keepdims=True) + EPS)
    return (center * inverse, inverse)


def norm_back(grad_y, normed, inverse, gain):
    scaled = grad_y * gain
    return inverse * (
        scaled
        - jnp.mean(scaled, -1, keepdims=True)
        - normed * jnp.mean(scaled * normed, -1, keepdims=True)
    )


def gelu_parts(values):
    bend = jnp.tanh(GELU_C * (values + GELU_K * values * values * values))
    return (0.5 * values * (1.0 + bend), bend)


def gelu_slope(values, bend):
    return 0.5 * (1.0 + bend) + 0.5 * values * (1.0 - bend * bend) * GELU_C * (
        1.0 + 3.0 * GELU_K * values * values
    )


def block_mask(q_pos, q_seg, key_seg, start, block):
    k_pos = start + jnp.arange(block, dtype=jnp.int32)
    seg_keys = lax.dynamic_slice_in_dim(key_seg, start, block, 1)
    mask = (k_pos[None, None, :] <= q_pos[None, :, None]) & (
        seg_keys[:, None, :] == q_seg[:, :, None]
    )
    return mask[:, None]


def block_scores(query, keys, q_pos, start, block, slope, scale):
    k_pos = start + jnp.arange(block, dtype=jnp.int32)
    dist = (q_pos[:, None] - k_pos[None, :]).astype(jnp.float32)
    score = jnp.einsum("sqhd,skhd->shqk", query, keys, preferred_element_type=jnp.float32)
    return score * scale - slope[None, :, None, None] * dist[None, None]


def attend_forward(query, kv_all, q_pos, q_seg, key_seg, slope):
    seqs, rows, heads, width = query.shape
    length = kv_all.shape[1]
    block = min(512, length)
    scale = 1.0 / math.sqrt(width)

    def step(carry, index):
        start = index * block
        mask = block_mask(q_pos, q_seg, key_seg, start, block)

        def work(state):
            acc, total = state
            pair = lax.dynamic_slice_in_dim(kv_all, start, block, 1).reshape(
                seqs, block, 2, heads, width
            )
            score = block_scores(query, pair[:, :, 0], q_pos, start, block, slope, scale)
            expo = jnp.where(mask, jnp.exp(jnp.where(mask, score, 0.0)), 0.0)
            acc = acc + jnp.einsum(
                "shqk,skhd->sqhd",
                expo.astype(jnp.bfloat16),
                pair[:, :, 1],
                preferred_element_type=jnp.float32,
            )
            return (acc, total + jnp.sum(expo, -1))

        return (lax.cond(jnp.any(mask), work, lambda state: state, carry), None)

    init = (jnp.zeros(query.shape, jnp.float32), jnp.zeros((seqs, heads, rows), jnp.float32))
    (acc, total), _ = lax.scan(step, init, jnp.arange(length // block, dtype=jnp.int32))
    ctx = (acc / jnp.transpose(total, (0, 2, 1))[..., None]).astype(jnp.bfloat16)
    return (ctx, jnp.log(total))


def attend_backward(query, kv_all, q_pos, q_seg, key_seg, slope, ctx, lse, dctx):
    seqs, rows, heads, width = query.shape
    length = kv_all.shape[1]
    block = min(512, length)
    scale = 1.0 / math.sqrt(width)
    delta = jnp.transpose(
        jnp.sum(dctx.astype(jnp.float32) * ctx.astype(jnp.float32), -1), (0, 2, 1)
    )

    def step(carry, index):
        start = index * block
        mask = block_mask(q_pos, q_seg, key_seg, start, block)

        def work(state):
            grad_q, grad_kv = state
            pair = lax.dynamic_slice_in_dim(kv_all, start, block, 1).reshape(
                seqs, block, 2, heads, width
            )
            score = block_scores(query, pair[:, :, 0], q_pos, start, block, slope, scale)
            prob = jnp.where(mask, jnp.exp(jnp.where(mask, score - lse[..., None], 0.0)), 0.0)
            grad_v = jnp.einsum(
                "shqk,sqhd->skhd",
                prob.astype(jnp.bfloat16),
                dctx,
                preferred_element_type=jnp.float32,
            )
            grad_p = jnp.einsum(
                "sqhd,skhd->shqk", dctx, pair[:, :, 1], preferred_element_type=jnp.float32
            )
            grad_s = (prob * (grad_p - delta[..., None])).astype(jnp.bfloat16)
            grad_q = (
                grad_q
                + jnp.einsum(
                    "shqk,skhd->sqhd", grad_s, pair[:, :, 0], preferred_element_type=jnp.float32
                )
                * scale
            )
            grad_k = (
                jnp.einsum("shqk,sqhd->skhd", grad_s, query, preferred_element_type=jnp.float32)
                * scale
            )
            piece = jnp.stack([grad_k, grad_v], 2).reshape(seqs, block, 2, heads * width)
            return (grad_q, lax.dynamic_update_slice_in_dim(grad_kv, piece, start, 1))

        return (lax.cond(jnp.any(mask), work, lambda state: state, carry), None)

    init = (
        jnp.zeros(query.shape, jnp.float32),
        jnp.zeros((seqs, length, 2, heads * width), jnp.float32),
    )
    (grad_q, grad_kv), _ = lax.scan(step, init, jnp.arange(length // block, dtype=jnp.int32))
    return (grad_q, grad_kv)


def per_device(hidden_in, segment_ids, gains, biases, w_qkv, w_out_t, w_up, w_down_t, grad_out):
    seqs, rows, width = hidden_in.shape
    layers = w_qkv.shape[0]
    cols = w_qkv.shape[3]
    ff_cols = w_up.shape[2]
    heads = cols // HEAD
    mp_count = lax.axis_size("mp")
    mp_index = lax.axis_index("mp")
    all_gains, all_biases = (
        lax.all_gather(gains, ("batch", "ctx", "mp"), axis=2, tiled=True),
        lax.all_gather(biases, ("batch", "ctx", "mp"), axis=2, tiled=True),
    )
    key_seg = lax.all_gather(segment_ids, "ctx", axis=1, tiled=True)
    q_pos = lax.axis_index("ctx") * rows + jnp.arange(rows, dtype=jnp.int32)
    head_ids = (mp_index * heads + jnp.arange(heads, dtype=jnp.int32)).astype(jnp.float32)
    slope = jnp.exp2(-8.0 * (head_ids + 1.0) / HEADS)
    own = (jnp.arange(width, dtype=jnp.int32) // cols == mp_index).astype(jnp.float32)
    full_ff = ff_cols * mp_count

    def place(values, offset, total):
        return lax.dynamic_update_slice_in_dim(jnp.zeros((total,), jnp.float32), values, offset, 0)

    def unpack(layer):
        vec = all_biases[layer]
        query_bias = lax.dynamic_slice_in_dim(vec[2], mp_index * cols, cols, 0)
        value_bias = lax.dynamic_slice_in_dim(vec[3], mp_index * cols, cols, 0)
        up_projection_bias = lax.dynamic_slice_in_dim(
            vec[6:].reshape(-1), mp_index * ff_cols, ff_cols, 0
        )
        return (vec, query_bias, value_bias, up_projection_bias)

    def forward_layer(layer, state, weights):
        query_weight, w_o, up_weight, w_d = weights
        vec, query_bias, value_bias, up_projection_bias = unpack(layer)
        normed1, _ = norm_parts(state)
        first_activation = (normed1 * all_gains[layer, 0] + vec[0]).astype(jnp.bfloat16)
        query_key_value = jnp.einsum(
            "bph,hue->bpue", first_activation, query_weight, preferred_element_type=jnp.float32
        )
        shift = jnp.stack([query_bias, jnp.zeros_like(query_bias), value_bias])
        qkv_bf = (query_key_value + shift).astype(jnp.bfloat16)
        kv_all = lax.all_gather(qkv_bf[:, :, 1:], "ctx", axis=1, tiled=True)
        query = qkv_bf[:, :, 0].reshape(seqs, rows, heads, HEAD)
        ctx, lse = attend_forward(query, kv_all, q_pos, segment_ids, key_seg, slope)
        ctx_flat = ctx.reshape(seqs, rows, cols)
        part = jnp.einsum("slc,oc->slo", ctx_flat, w_o, preferred_element_type=jnp.float32)
        mid = state + lax.psum(part, "mp") + vec[4]
        normed2, _ = norm_parts(mid)
        second_activation = (normed2 * all_gains[layer, 1] + vec[1]).astype(jnp.bfloat16)
        up_projected = (
            jnp.einsum(
                "nhz,zb->nhb", second_activation, up_weight, preferred_element_type=jnp.float32
            )
            + up_projection_bias
        )
        act, _ = gelu_parts(up_projected)
        act_bf = act.astype(jnp.bfloat16)
        down = jnp.einsum("slf,of->slo", act_bf, w_d, preferred_element_type=jnp.float32)
        result = mid + lax.psum(down, "mp") + vec[5]
        return (
            result,
            (
                state,
                first_activation,
                qkv_bf,
                kv_all,
                ctx_flat,
                lse,
                mid,
                second_activation,
                up_projected,
                act_bf,
            ),
        )

    state = hidden_in.astype(jnp.float32)
    saves = []
    for layer in range(layers):
        weights = (
            lax.all_gather(w_qkv[layer], ("batch", "ctx"), axis=0, tiled=True),
            lax.all_gather(w_out_t[layer], ("batch", "ctx"), axis=0, tiled=True),
            lax.all_gather(w_up[layer], ("batch", "ctx"), axis=0, tiled=True),
            lax.all_gather(w_down_t[layer], ("batch", "ctx"), axis=0, tiled=True),
        )
        state, saved = forward_layer(layer, state, weights)
        saves.append((weights, saved))
    output = state.astype(jnp.bfloat16)
    grad = grad_out.astype(jnp.float32)
    gain_rows = [None] * layers
    bias_rows = [None] * layers
    matrix_grads = [None] * layers
    for layer in reversed(range(layers)):
        kept_weights, saved = saves[layer]
        (
            x_in,
            first_activation,
            qkv_bf,
            kv_kept,
            ctx_flat,
            lse,
            mid,
            second_activation,
            up_projected,
            act_bf,
        ) = saved
        query_weight, w_o, up_weight, w_d = (
            lax.all_gather(w_qkv[layer], ("batch", "ctx"), axis=0, tiled=True),
            lax.all_gather(w_out_t[layer], ("batch", "ctx"), axis=0, tiled=True),
            lax.all_gather(w_up[layer], ("batch", "ctx"), axis=0, tiled=True),
            lax.all_gather(w_down_t[layer], ("batch", "ctx"), axis=0, tiled=True),
        )
        kv_all = lax.all_gather(qkv_bf[:, :, 1:], "ctx", axis=1, tiled=True)
        gain1 = all_gains[layer, 0]
        gain2 = all_gains[layer, 1]
        grad_bf = grad.astype(jnp.bfloat16)
        grad_bd = jnp.sum(grad, (0, 1))
        grad_wd = jnp.einsum("slo,slf->of", grad_bf, act_bf, preferred_element_type=jnp.float32)
        dact = jnp.einsum("slo,of->slf", grad_bf, w_d, preferred_element_type=jnp.float32)
        _, bend = gelu_parts(up_projected)
        dup = dact * gelu_slope(up_projected, bend)
        grad_bu = jnp.sum(dup, (0, 1))
        up_gradient_half_precision = dup.astype(jnp.bfloat16)
        up_weight_gradient = jnp.einsum(
            "qwi,qwn->in",
            second_activation,
            up_gradient_half_precision,
            preferred_element_type=jnp.float32,
        )
        da2 = lax.psum(
            jnp.einsum(
                "cju,xu->cjx",
                up_gradient_half_precision,
                up_weight,
                preferred_element_type=jnp.float32,
            ),
            "mp",
        )
        normed2, inverse2 = norm_parts(mid)
        grad_g2 = jnp.sum(da2 * normed2, (0, 1))
        grad_b2 = jnp.sum(da2, (0, 1))
        gx2 = grad + norm_back(da2, normed2, inverse2, gain2)
        grad_bo = jnp.sum(gx2, (0, 1))
        gx2_bf = gx2.astype(jnp.bfloat16)
        grad_wo = jnp.einsum("slo,slc->oc", gx2_bf, ctx_flat, preferred_element_type=jnp.float32)
        dctx = jnp.einsum("slo,oc->slc", gx2_bf, w_o, preferred_element_type=jnp.float32).astype(
            jnp.bfloat16
        )
        query = qkv_bf[:, :, 0].reshape(seqs, rows, heads, HEAD)
        ctx_heads = ctx_flat.reshape(seqs, rows, heads, HEAD)
        dctx_heads = dctx.reshape(seqs, rows, heads, HEAD)
        grad_q, grad_kv_terms = attend_backward(
            query, kv_all, q_pos, segment_ids, key_seg, slope, ctx_heads, lse, dctx_heads
        )
        grad_kv = lax.psum_scatter(grad_kv_terms, "ctx", scatter_dimension=1, tiled=True)
        grad_qf = grad_q.reshape(seqs, rows, cols)
        grad_bq = jnp.sum(grad_qf, (0, 1))
        value_bias_gradient = jnp.sum(grad_kv[:, :, 1], (0, 1))
        packed_projection_gradient = jnp.concatenate([grad_qf[:, :, None], grad_kv], 2).astype(
            jnp.bfloat16
        )
        query_weight_gradient = jnp.einsum(
            "ebz,ebpy->zpy",
            first_activation,
            packed_projection_gradient,
            preferred_element_type=jnp.float32,
        )
        da1 = lax.psum(
            jnp.einsum(
                "aewu,vwu->aev",
                packed_projection_gradient,
                query_weight,
                preferred_element_type=jnp.float32,
            ),
            "mp",
        )
        normed1, inverse1 = norm_parts(x_in)
        grad_g1 = jnp.sum(da1 * normed1, (0, 1))
        grad_b1 = jnp.sum(da1, (0, 1))
        grad = gx2 + norm_back(da1, normed1, inverse1, gain1)
        gain_rows[layer] = jnp.stack([grad_g1 * own, grad_g2 * own])
        head_rows = jnp.stack(
            [
                grad_b1 * own,
                grad_b2 * own,
                place(grad_bq, mp_index * cols, width),
                place(value_bias_gradient, mp_index * cols, width),
                grad_bo * own,
                grad_bd * own,
            ]
        )
        unit_rows = place(grad_bu, mp_index * ff_cols, full_ff).reshape(full_ff // width, width)
        bias_rows[layer] = jnp.concatenate([head_rows, unit_rows], 0)
        matrix_grads[layer] = (
            lax.psum_scatter(
                query_weight_gradient.astype(jnp.bfloat16),
                ("batch", "ctx"),
                scatter_dimension=0,
                tiled=True,
            ).astype(jnp.float32),
            lax.psum_scatter(
                grad_wo.astype(jnp.bfloat16), ("batch", "ctx"), scatter_dimension=0, tiled=True
            ).astype(jnp.float32),
            lax.psum_scatter(
                up_weight_gradient.astype(jnp.bfloat16),
                ("batch", "ctx"),
                scatter_dimension=0,
                tiled=True,
            ).astype(jnp.float32),
            lax.psum_scatter(
                grad_wd.astype(jnp.bfloat16), ("batch", "ctx"), scatter_dimension=0, tiled=True
            ).astype(jnp.float32),
        )
    grad_gains, grad_biases = (
        lax.psum_scatter(
            jnp.stack(gain_rows), ("batch", "ctx", "mp"), scatter_dimension=2, tiled=True
        ),
        lax.psum_scatter(
            jnp.stack(bias_rows), ("batch", "ctx", "mp"), scatter_dimension=2, tiled=True
        ),
    )
    grad_qkv = jnp.stack([item[0] for item in matrix_grads])
    grad_attn_out = jnp.stack([item[1] for item in matrix_grads])
    grad_up = jnp.stack([item[2] for item in matrix_grads])
    grad_down = jnp.stack([item[3] for item in matrix_grads])
    return (
        output,
        grad.astype(jnp.bfloat16),
        grad_gains,
        grad_biases,
        grad_qkv,
        grad_attn_out,
        grad_up,
        grad_down,
    )


def solution(mesh):
    in_specs = (
        P("batch", "ctx", None),
        P("batch", "ctx"),
        P(None, None, ("batch", "ctx", "mp")),
        P(None, None, ("batch", "ctx", "mp")),
        P(None, ("batch", "ctx"), None, "mp"),
        P(None, ("batch", "ctx"), "mp"),
        P(None, ("batch", "ctx"), "mp"),
        P(None, ("batch", "ctx"), "mp"),
        P("batch", "ctx", None),
    )
    out_specs = (
        P("batch", "ctx", None),
        P("batch", "ctx", None),
        P(None, None, ("batch", "ctx", "mp")),
        P(None, None, ("batch", "ctx", "mp")),
        P(None, ("batch", "ctx"), None, "mp"),
        P(None, ("batch", "ctx"), "mp"),
        P(None, ("batch", "ctx"), "mp"),
        P(None, ("batch", "ctx"), "mp"),
    )
    return jax.shard_map(
        per_device, mesh=mesh, in_specs=in_specs, out_specs=out_specs, check_vma=False
    )
```

profile of v0, /device:TPU:0, one launch (start us, length us, event | category | flops | bytes accessed | tf_op | source)
XLA Modules:
  0.0 1558.1 jit_solution(14924374231961429402)
XLA Ops:
  10.7 74.2 %all_gather.51 = bf16[2,10,1024]{1,0,2:T(2,128)(2,1)S(1)} all-gather(bf16[2,10,32]{1,0,2:T(2,128)(2,1)S(1)} %copy.109), channel_id=1, replica_groups=mesh['batch'=2,'ctx'=4,'mp'=4] {'batch','ctx','mp'}, dimensions={2}, use_global_device_ids=true | all-gather | bytes 42240 | tf_op jit(solution)/shard_map/all_gather | solution.py:153
  84.8 2.5 fusion.155
  89.5 68.0 %all_gather.50 = bf16[2,2,1024]{1,0,2:T(2,128)(2,1)S(1)} all-gather(bf16[2,2,32]{1,0,2:T(2,128)(2,1)S(1)} %copy.108), channel_id=1, replica_groups=mesh['batch'=2,'ctx'=4,'mp'=4] {'batch','ctx','mp'}, dimensions={2}, use_global_device_ids=true | all-gather | bytes 8448 | tf_op jit(solution)/shard_map/all_gather | solution.py:152
  158.0 18.2 %fusion.103 = (f32[1024]{0:T(1024)S(1)}, f32[1024]{0:T(1024)S(1)}, f32[1024]{0:T(1024)S(1)}, f32[1024]{0:T(1024)S(1)}) fusion(bf16[2,2,1024]{1,0,2:T(2,128)(2,1)S(1)} %all_gather.50), kind=kLoop, calls=%fused_computation.161 | loop fusion | flops 4096 | bytes 24576 | tf_op jit(solution)/shard_map/mul | solution.py:191
  176.3 24.6 %fusion.101 = (f32[1024]{0:T(1024)}, f32[1024]{0:T(1024)}, f32[1024]{0:T(1024)}, f32[1024]{0:T(1024)S(1)}, f32[1024]{0:T(1024)S(1)}, /*index=5*/f32[1024]{0:T(1024)S(1)}, f32[1024]{0:T(1024)S(1)}, f32[1024]{0:T(1024)S(1)}) fusion(bf16[2,10,1024]{1,0,2:T(2,128)(2,1)S(1)} %all_gather.51), kind=kLoop, calls=%fused_computation.157 | loop fusion | flops 8192 | bytes 49152 | tf_op jit(solution)/shard_map/add | solution.py:201
  203.8 5.1 all_gather.49
  212.8 9.1 all-gather.1
  222.8 6.8 conditional.4
  226.6 2.5 fusion.148
  235.5 45.8 %all-reduce.9.cloned.1.call-done = f32[2,128,1024]{2,1,0:T(8,128)} async-done(((f32[2,128,1024]{2,1,0:T(8,128)}), f32[2,128,1024]{2,1,0:T(8,128)}) %all-reduce.9.cloned.1.call-update) | async-done | bytes 1048592 | tf_op jit(solution)/shard_map/psum | solution.py:189
  283.0 27.7 %all-gather.23.cloned.1.call-done = bf16[1,1024,1024]{2,1,0:T(8,128)(2,1)} async-done(((bf16[1,128,1024]{2,1,0:T(8,128)(2,1)}), bf16[1,1024,1024]{2,1,0:T(8,128)(2,1)}) %all-gather.23.cloned.1.call-update) | async-done | bytes 2097168 | tf_op jit(solution)/shard_map/all_gather | solution.py:224
  310.6 2.4 fusion.47
  313.0 27.7 %all-gather.25.cloned.1.call-done = bf16[1,1024,1024]{2,1,0:T(8,128)(2,1)} async-done(((bf16[1,128,1024]{2,1,0:T(8,128)(2,1)}), bf16[1,1024,1024]{2,1,0:T(8,128)(2,1)}) %all-gather.25.cloned.1.call-update) | async-done | bytes 2097168 | tf_op jit(solution)/shard_map/all_gather | solution.py:225
  340.8 3.4 fusion.26
  345.0 51.3 %all-reduce.11.cloned.1.call-done = f32[2,128,1024]{2,1,0:T(8,128)} async-done(((f32[2,128,1024]{2,1,0:T(8,128)}), f32[2,128,1024]{2,1,0:T(8,128)}) %all-reduce.11.cloned.1.call-update) | async-done | bytes 1048592 | tf_op jit(solution)/shard_map/psum | solution.py:201
  397.9 25.1 %all-gather.27.cloned.1.call-done = bf16[1,1024,3,256]{3,1,2,0:T(8,128)(2,1)} async-done(((bf16[1,128,3,256]{3,1,2,0:T(8,128)(2,1)}), bf16[1,1024,3,256]{3,1,2,0:T(8,128)(2,1)}) %all-gather.27.cloned.1.call-update) | async-done | bytes 1572880 | tf_op jit(solution)/shard_map/all_gather | solution.py:222
  425.9 9.8 all-gather.5
  436.5 6.2 all-gather.19.cloned.1.call-done
  442.7 7.7 conditional.5
  447.4 2.5 fusion.149
  454.4 49.4 %all-reduce.13.cloned.1.call-done = f32[2,128,1024]{2,1,0:T(8,128)} async-done(((f32[2,128,1024]{2,1,0:T(8,128)}), f32[2,128,1024]{2,1,0:T(8,128)}) %all-reduce.13.cloned.1.call-update) | async-done | bytes 1048592 | tf_op jit(solution)/shard_map/psum | solution.py:189
  505.6 27.1 %all-gather.29.cloned.1.call-done = bf16[1,1024,1024]{2,1,0:T(8,128)(2,1)} async-done(((bf16[1,128,1024]{2,1,0:T(8,128)(2,1)}), bf16[1,1024,1024]{2,1,0:T(8,128)(2,1)}) %all-gather.29.cloned.1.call-update) | async-done | bytes 2097168 | tf_op jit(solution)/shard_map/all_gather | solution.py:224
  532.7 3.3 fusion.53
  536.0 26.9 %all-gather.31.cloned.1.call-done = bf16[1,1024,1024]{2,1,0:T(8,128)(2,1)} async-done(((bf16[1,128,1024]{2,1,0:T(8,128)(2,1)}), bf16[1,1024,1024]{2,1,0:T(8,128)(2,1)}) %all-gather.31.cloned.1.call-update) | async-done | bytes 2097168 | tf_op jit(solution)/shard_map/all_gather | solution.py:225
  563.0 3.9 fusion.158
  571.7 49.8 %all-reduce.15.cloned.1.call-done = f32[2,128,1024]{2,1,0:T(8,128)} async-done(((f32[2,128,1024]{2,1,0:T(8,128)}), f32[2,128,1024]{2,1,0:T(8,128)}) %all-reduce.15.cloned.1.call-update) | async-done | bytes 1048592 | tf_op jit(solution)/shard_map/psum | solution.py:271
  621.5 2.4 multiply_reduce_fusion
  629.7 16.5 %conditional.6 = (f32[2,512,2,256]{1,3,0,2:T(8,128)}, f32[1,256]{1,0:T(1,128)}, bf16[2,128,1,256]{3,1,2,0:T(8,128)(2,1)S(1)}) conditional(s32[]{:T(128)} %convert_element_type.234, (f32[2,512,2,256]{1,3,0,2:T(8,128)}, f32[2,128,4,64]{1,3,2,0:T(8,128)S(1)}) %tuple.89, (pred[2,1,128,512]{3,2,0,1:T(8,128)(4,1)}, ...), branch_computations={%region_23.24_spmd.clone, %region_24.25_spmd.clone} | conditional | flops 341704448 | bytes 28077692 | solution.py:133
  634.7 2.4 exponential_select_fusion.3
  642.4 3.1 pad_maximum_fusion.1
  646.1 3.0 copy.120
  649.2 30.6 %reduce-scatter.17.cloned.1.call-done = f32[2,128,2,256]{3,1,2,0:T(8,128)} async-done(((f32[2,512,2,256]{3,1,2,0:T(8,128)}), f32[2,128,2,256]{3,1,2,0:T(8,128)}) %reduce-scatter.17.cloned.1.call-update) | async-done | bytes 524304 | tf_op jit(solution)/shard_map/reduce_scatter | solution.py:296
  681.6 3.0 fusion.44
  684.6 52.0 %all-reduce.17.cloned.1.call-done = f32[2,128,1024]{2,1,0:T(8,128)} async-done(((f32[2,128,1024]{2,1,0:T(8,128)}), f32[2,128,1024]{2,1,0:T(8,128)}) %all-reduce.17.cloned.1.call-update) | async-done | bytes 1048592 | tf_op jit(solution)/shard_map/psum | solution.py:309
  736.6 2.5 multiply_reduce_fusion.1
  746.0 50.7 %all-reduce.19.cloned.1.call-done = f32[2,128,1024]{2,1,0:T(8,128)} async-done(((f32[2,128,1024]{2,1,0:T(8,128)}), f32[2,128,1024]{2,1,0:T(8,128)}) %all-reduce.19.cloned.1.call-update) | async-done | bytes 1048592 | tf_op jit(solution)/shard_map/psum | solution.py:271
  796.7 2.4 multiply_reduce_fusion.2
  804.7 15.0 conditional.7
  807.1 2.4 copy.123
  809.5 2.3 exponential_select_fusion.2
  816.6 3.1 pad_maximum_fusion
  819.8 2.9 copy.124
  822.8 3.7 fusion.18
  826.5 26.8 %reduce-scatter.19.cloned.1.call-done = f32[2,128,2,256]{3,1,2,0:T(8,128)} async-done(((f32[2,512,2,256]{3,1,2,0:T(8,128)}), f32[2,128,2,256]{3,1,2,0:T(8,128)}) %reduce-scatter.19.cloned.1.call-update) | async-done | bytes 524304 | tf_op jit(solution)/shard_map/reduce_scatter | solution.py:296
  855.1 3.0 fusion.41
  858.5 2.4 fusion.60
  860.9 2.4 fusion.59
  863.4 3.3 bitcast_convert_fusion.2
  866.9 3.2 bitcast_convert_fusion.3
  871.2 3.4 fusion.32
  875.8 3.4 bitcast_convert_fusion.1
  882.2 62.4 %all-reduce.21.cloned.1.call-done = (f32[2,128,1024]{2,1,0:T(8,128)}, f32[2,128,1024]{2,1,0:T(8,128)}) async-done(((f32[2,128,1024]{2,1,0:T(8,128)}, f32[2,128,1024]{2,1,0:T(8,128)}), (f32[2,128,1024]{2,1,0:T(8,128)}, f32[2,128,1024]{2,1,0:T(8,128)})) %all-reduce.21.cloned.1.call-update) | async-done | bytes 2097168 | tf_op jit(solution)/shard_map/psum | solution.py:201
  947.6 2.6 reshape.647
  951.8 2.7 reshape.649
  958.7 22.5 %reduce-scatter.27.cloned.1.call-done = bf16[128,256]{1,0:T(8,128)(2,1)} async-done(((bf16[1024,256]{1,0:T(8,128)(2,1)}), bf16[128,256]{1,0:T(8,128)(2,1)}) %reduce-scatter.27.cloned.1.call-update) | async-done | bytes 65552 | tf_op jit(solution)/shard_map/reduce_scatter | solution.py:342
  981.2 37.8 %reduce-scatter.25.cloned.1.call-done = bf16[128,256]{1,0:T(8,128)(2,1)} async-done(((bf16[1024,256]{1,0:T(8,128)(2,1)}), bf16[128,256]{1,0:T(8,128)(2,1)}) %reduce-scatter.25.cloned.1.call-update) | async-done | bytes 65552 | tf_op jit(solution)/shard_map/reduce_scatter | solution.py:342
  1020.6 42.7 %reduce-scatter.31.cloned.1.call-done = bf16[128,1024]{1,0:T(8,128)(2,1)} async-done(((bf16[1024,1024]{1,0:T(8,128)(2,1)}), bf16[128,1024]{1,0:T(8,128)(2,1)}) %reduce-scatter.31.cloned.1.call-update) | async-done | bytes 262160 | tf_op jit(solution)/shard_map/reduce_scatter | solution.py:345
  1063.3 44.4 %reduce-scatter.29.cloned.1.call-done = bf16[128,1024]{1,0:T(8,128)(2,1)} async-done(((bf16[1024,1024]{1,0:T(8,128)(2,1)}), bf16[128,1024]{1,0:T(8,128)(2,1)}) %reduce-scatter.29.cloned.1.call-update) | async-done | bytes 262160 | tf_op jit(solution)/shard_map/reduce_scatter | solution.py:345
  1109.8 42.4 %reduce-scatter.35.cloned.1.call-done = bf16[128,1024]{1,0:T(8,128)(2,1)} async-done(((bf16[1024,1024]{1,0:T(8,128)(2,1)}), bf16[128,1024]{1,0:T(8,128)(2,1)}) %reduce-scatter.35.cloned.1.call-update) | async-done | bytes 262160 | tf_op jit(solution)/shard_map/reduce_scatter | solution.py:351
  1152.1 44.4 %reduce-scatter.33.cloned.1.call-done = bf16[128,1024]{1,0:T(8,128)(2,1)} async-done(((bf16[1024,1024]{1,0:T(8,128)(2,1)}), bf16[128,1024]{1,0:T(8,128)(2,1)}) %reduce-scatter.33.cloned.1.call-update) | async-done | bytes 262160 | tf_op jit(solution)/shard_map/reduce_scatter | solution.py:351
  1201.1 134.4 %reduce-scatter.37.cloned.1.call-done = f32[32,4]{1,0:T(8,128)} async-done(((f32[1024,4]{1,0:T(8,128)}), f32[32,4]{1,0:T(8,128)}) %reduce-scatter.37.cloned.1.call-update) | async-done | bytes 528
  1337.0 133.0 %reduce-scatter.39.cloned.1.call-done = f32[32,20]{1,0:T(8,128)} async-done(((f32[1024,20]{1,0:T(8,128)}), f32[32,20]{1,0:T(8,128)}) %reduce-scatter.39.cloned.1.call-update) | async-done | bytes 2576
  1471.5 36.1 %reduce-scatter.23.cloned.1.call-done = bf16[128,3,256]{2,0,1:T(8,128)(2,1)} async-done(((bf16[1024,3,256]{2,0,1:T(8,128)(2,1)}), bf16[128,3,256]{2,0,1:T(8,128)(2,1)}) %reduce-scatter.23.cloned.1.call-update) | async-done | bytes 196624 | tf_op jit(solution)/shard_map/reduce_scatter | solution.py:336
  1507.6 41.5 %reduce-scatter.21.cloned.1.call-done = bf16[128,3,256]{2,0,1:T(8,128)(2,1)} async-done(((bf16[1024,3,256]{2,0,1:T(8,128)(2,1)}), bf16[128,3,256]{2,0,1:T(8,128)(2,1)}) %reduce-scatter.21.cloned.1.call-update) | async-done | bytes 196624 | tf_op jit(solution)/shard_map/reduce_scatter | solution.py:336
  (422 shorter events, 113.4 us)
Async XLA Ops:
  7.2 193.7 %all-gather.21.cloned.1.call-start = ((), (), s32[]{:S(2)}) async-start(), calls=%async_computation.30 | async-start | bytes 1769472 | tf_op jit(solution)/shard_map/all_gather | solution.py:222
  9.0 213.7 %all-gather.17.cloned.1.call-start = ((), (), s32[]{:S(2)}) async-start(), calls=%async_computation.12 | async-start | bytes 1310720 | tf_op jit(solution)/shard_map/all_gather | solution.py:184
  84.8 72.7 %copy-start.4 = (bf16[2,128,1024]{2,1,0:T(8,128)(2,1)S(1)}, bf16[2,128,1024]{2,1,0:T(8,128)(2,1)}, u32[]{:S(2)}) copy-start(bf16[2,128,1024]{2,1,0:T(8,128)(2,1)} %param.17) | copy-start | bytes 1572868
  157.7 43.2 %copy-start.63 = (f32[2,128]{1,0:T(2,128)}, f32[2,128]{1,0:T(2,128)S(1)}, u32[]{:S(2)}) copy-start(f32[2,128]{1,0:T(2,128)S(1)} %broadcast_multiply_fusion.15) | copy-start | bytes 3076
  158.0 42.9 %copy-start.89 = (f32[2,128]{1,0:T(2,128)}, f32[2,128]{1,0:T(2,128)S(1)}, u32[]{:S(2)}) copy-start(f32[2,128]{1,0:T(2,128)S(1)} %add_rsqrt_fusion.3) | copy-start | bytes 3076
  176.2 24.6 %copy-start.52 = (f32[1024]{0:T(1024)}, f32[1024]{0:T(1024)S(1)}, u32[]{:S(2)}) copy-start(f32[1024]{0:T(1024)S(1)} %get-tuple-element.615) | copy-start | bytes 12292
  176.2 246.8 %copy-start.54 = (f32[1024]{0:T(1024)}, f32[1024]{0:T(1024)S(1)}, u32[]{:S(2)}) copy-start(f32[1024]{0:T(1024)S(1)} %get-tuple-element.613) | copy-start | bytes 12292
  200.9 109.8 %copy-start.84 = (f32[1024]{0:T(1024)}, f32[1024]{0:T(1024)S(1)}, u32[]{:S(2)}) copy-start(f32[1024]{0:T(1024)S(1)} %get-tuple-element.609) | copy-start | bytes 12292
  200.9 222.1 %copy-start.102 = (f32[1024]{0:T(1024)}, f32[1024]{0:T(1024)S(1)}, u32[]{:S(2)}) copy-start(f32[1024]{0:T(1024)S(1)} %get-tuple-element.607) | copy-start | bytes 12292
  200.9 11.9 copy-start.49
  203.8 77.5 %all-reduce.9.cloned.1.call-start = ((), (), s32[]{:S(2)}) async-start(), calls=%async_computation.13 | async-start | bytes 2097152 | tf_op jit(solution)/shard_map/psum | solution.py:189
  221.9 7.7 copy-start.9
  231.0 79.6 %all-gather.23.cloned.1.call-start = ((), (), s32[]{:S(2)}) async-start(), calls=%async_computation.31 | async-start | bytes 2359296 | tf_op jit(solution)/shard_map/all_gather | solution.py:224
  231.9 108.8 %all-gather.25.cloned.1.call-start = ((), (), s32[]{:S(2)}) async-start(), calls=%async_computation.32 | async-start | bytes 2359296 | tf_op jit(solution)/shard_map/all_gather | solution.py:225
  232.8 163.4 %all-reduce.11.cloned.1.call-start = ((), (), s32[]{:S(2)}) async-start(), calls=%async_computation.14 | async-start | bytes 2097152 | tf_op jit(solution)/shard_map/psum | solution.py:201
  282.7 30.3 %copy-start.56 = (f32[2,128]{1,0:T(2,128)}, f32[2,128]{1,0:T(2,128)S(1)}, u32[]{:S(2)}) copy-start(f32[2,128]{1,0:T(2,128)S(1)} %broadcast_multiply_fusion.14) | copy-start | bytes 3076
  283.0 30.0 %copy-start.65 = (f32[2,128]{1,0:T(2,128)}, f32[2,128]{1,0:T(2,128)S(1)}, u32[]{:S(2)}) copy-start(f32[2,128]{1,0:T(2,128)S(1)} %add_rsqrt_fusion.2) | copy-start | bytes 3076
  313.0 31.1 %copy-start.38 = (f32[2,128,1024]{2,1,0:T(8,128)}, f32[2,128,1024]{2,1,0:T(8,128)S(1)}, u32[]{:S(2)}) copy-start(f32[2,128,1024]{2,1,0:T(8,128)S(1)} %fusion.47) | copy-start | bytes 3145732
  344.2 78.8 %all-gather.27.cloned.1.call-start = ((), (), s32[]{:S(2)}) async-start(), calls=%async_computation.33 | async-start | bytes 1769472 | tf_op jit(solution)/shard_map/all_gather | solution.py:222
  344.9 97.7 %all-gather.19.cloned.1.call-start = ((), (), s32[]{:S(2)}) async-start(), calls=%async_computation.15 | async-start | bytes 1310720 | tf_op jit(solution)/shard_map/all_gather | solution.py:184
  397.7 27.4 %copy-start.80 = (f32[2,128]{1,0:T(2,128)}, f32[2,128]{1,0:T(2,128)S(1)}, u32[]{:S(2)}) copy-start(f32[2,128]{1,0:T(2,128)S(1)} %broadcast_multiply_fusion.13) | copy-start | bytes 3076
  397.9 27.9 %copy-start.91 = (f32[2,128]{1,0:T(2,128)}, f32[2,128]{1,0:T(2,128)S(1)}, u32[]{:S(2)}) copy-start(f32[2,128]{1,0:T(2,128)S(1)} %add_rsqrt_fusion.1) | copy-start | bytes 3076
  425.8 78.1 %all-reduce.13.cloned.1.call-start = ((), (), s32[]{:S(2)}) async-start(), calls=%async_computation.16 | async-start | bytes 2097152 | tf_op jit(solution)/shard_map/psum | solution.py:189
  435.7 14.8 copy-start.11
  442.7 4.8 copy-start.51
  450.4 53.5 %copy-start.88 = (f32[1024]{0:T(1024)S(1)}, f32[1024]{0:T(1024)}, u32[]{:S(2)}) copy-start(f32[1024]{0:T(1024)} %get-tuple-element.606) | copy-start | bytes 12292
  450.5 53.4 %copy-start.31 = (bf16[2,128,4,64]{1,3,2,0:T(8,128)(2,1)}, bf16[2,128,4,64]{1,3,2,0:T(8,128)(2,1)S(1)}, u32[]{:S(2)}) copy-start(bf16[2,128,4,64]{1,3,2,0:T(8,128)(2,1)S(1)} %divide_convert_fusion) | copy-start | bytes 393220
  451.8 80.9 %all-gather.29.cloned.1.call-start = ((), (), s32[]{:S(2)}) async-start(), calls=%async_computation.34 | async-start | bytes 2359296 | tf_op jit(solution)/shard_map/all_gather | solution.py:224
  452.4 110.6 %all-gather.31.cloned.1.call-start = ((), (), s32[]{:S(2)}) async-start(), calls=%async_computation.35 | async-start | bytes 2359296 | tf_op jit(solution)/shard_map/all_gather | solution.py:225
  453.1 168.3 %all-reduce.15.cloned.1.call-start = ((), (), s32[]{:S(2)}) async-start(), calls=%async_computation.17 | async-start | bytes 2097152 | tf_op jit(solution)/shard_map/psum | solution.py:271
  503.9 28.8 %copy-start.86 = (f32[1024]{0:T(1024)S(1)}, f32[1024]{0:T(1024)}, u32[]{:S(2)}) copy-start(f32[1024]{0:T(1024)} %get-tuple-element.605) | copy-start | bytes 12292
  505.3 118.6 %copy-start.59 = (f32[2,128]{1,0:T(2,128)}, f32[2,128]{1,0:T(2,128)S(1)}, u32[]{:S(2)}) copy-start(f32[2,128]{1,0:T(2,128)S(1)} %broadcast_multiply_fusion.12) | copy-start | bytes 3076
  505.6 118.3 %copy-start.68 = (f32[2,128]{1,0:T(2,128)}, f32[2,128]{1,0:T(2,128)S(1)}, u32[]{:S(2)}) copy-start(f32[2,128]{1,0:T(2,128)S(1)} %add_rsqrt_fusion) | copy-start | bytes 3076
  569.4 110.3 %reduce-scatter.17.cloned.1.call-start = ((), (), s32[]{:S(2)}) async-start(), calls=%async_computation.18 | async-start | bytes 2621440 | tf_op jit(solution)/shard_map/reduce_scatter | solution.py:296
  646.1 34.7 %copy-start.43 = (bf16[2,128,1,256]{3,1,2,0:T(8,128)(2,1)}, bf16[2,128,1,256]{3,1,2,0:T(8,128)(2,1)S(1)}, u32[]{:S(2)}) copy-start(bf16[2,128,1,256]{3,1,2,0:T(8,128)(2,1)S(1)} %get-tuple-element.586) | copy-start | bytes 393220
  649.2 87.4 %all-reduce.17.cloned.1.call-start = ((), (), s32[]{:S(2)}) async-start(), calls=%async_computation.19 | async-start | bytes 2097152 | tf_op jit(solution)/shard_map/psum | solution.py:309
  680.9 55.7 %copy-start.55 = (f32[1024]{0:T(1024)S(1)}, f32[1024]{0:T(1024)}, u32[]{:S(2)}) copy-start(f32[1024]{0:T(1024)} %copy-done.54) | copy-start | bytes 12292
  684.5 54.5 %copy-start.81 = (f32[2,128]{1,0:T(2,128)S(1)}, f32[2,128]{1,0:T(2,128)}, u32[]{:S(2)}) copy-start(f32[2,128]{1,0:T(2,128)} %copy-done.80) | copy-start | bytes 3076
  684.5 54.5 %copy-start.92 = (f32[2,128]{1,0:T(2,128)S(1)}, f32[2,128]{1,0:T(2,128)}, u32[]{:S(2)}) copy-start(f32[2,128]{1,0:T(2,128)} %copy-done.91) | copy-start | bytes 3076
  684.6 112.1 %all-reduce.19.cloned.1.call-start = ((), (), s32[]{:S(2)}) async-start(), calls=%async_computation.20 | async-start | bytes 2097152 | tf_op jit(solution)/shard_map/psum | solution.py:271
  743.6 53.1 %copy-start.57 = (f32[2,128]{1,0:T(2,128)S(1)}, f32[2,128]{1,0:T(2,128)}, u32[]{:S(2)}) copy-start(f32[2,128]{1,0:T(2,128)} %copy-done.56) | copy-start | bytes 3076
  743.6 53.1 %copy-start.66 = (f32[2,128]{1,0:T(2,128)S(1)}, f32[2,128]{1,0:T(2,128)}, u32[]{:S(2)}) copy-start(f32[2,128]{1,0:T(2,128)} %copy-done.65) | copy-start | bytes 3076
  745.4 108.0 %reduce-scatter.19.cloned.1.call-start = ((), (), s32[]{:S(2)}) async-start(), calls=%async_computation.21 | async-start | bytes 2621440 | tf_op jit(solution)/shard_map/reduce_scatter | solution.py:296
  819.8 34.7 %copy-start.45 = (bf16[2,128,1,256]{3,1,2,0:T(8,128)(2,1)}, bf16[2,128,1,256]{3,1,2,0:T(8,128)(2,1)S(1)}, u32[]{:S(2)}) copy-start(bf16[2,128,1,256]{3,1,2,0:T(8,128)(2,1)S(1)} %get-tuple-element.587) | copy-start | bytes 393220
  822.7 121.8 %all-reduce.21.cloned.1.call-start = ((), (), s32[]{:S(2)}) async-start(), calls=%async_computation.38 | async-start | bytes 4194304 | tf_op jit(solution)/shard_map/psum | solution.py:201
  858.2 5.2 copy-start.60
  858.2 5.2 copy-start.69
  858.2 5.2 copy-start.87
  858.2 123.0 %reduce-scatter.27.cloned.1.call-start = ((), (), s32[]{:S(2)}) async-start(), calls=%async_computation.25 | async-start | bytes 589824 | tf_op jit(solution)/shard_map/reduce_scatter | solution.py:342
  860.9 158.1 %reduce-scatter.25.cloned.1.call-start = ((), (), s32[]{:S(2)}) async-start(), calls=%async_computation.24 | async-start | bytes 589824 | tf_op jit(solution)/shard_map/reduce_scatter | solution.py:342
  863.3 199.9 %reduce-scatter.31.cloned.1.call-start = ((), (), s32[]{:S(2)}) async-start(), calls=%async_computation.27 | async-start | bytes 2359296 | tf_op jit(solution)/shard_map/reduce_scatter | solution.py:345
  866.8 240.9 %reduce-scatter.29.cloned.1.call-start = ((), (), s32[]{:S(2)}) async-start(), calls=%async_computation.26 | async-start | bytes 2359296 | tf_op jit(solution)/shard_map/reduce_scatter | solution.py:345
  870.1 282.0 %reduce-scatter.35.cloned.1.call-start = ((), (), s32[]{:S(2)}) async-start(), calls=%async_computation.29 | async-start | bytes 2359296 | tf_op jit(solution)/shard_map/reduce_scatter | solution.py:351
  874.6 322.0 %reduce-scatter.33.cloned.1.call-start = ((), (), s32[]{:S(2)}) async-start(), calls=%async_computation.28 | async-start | bytes 2359296 | tf_op jit(solution)/shard_map/reduce_scatter | solution.py:351
  879.3 65.2 %copy-start.5 = (bf16[2,128,1024]{2,1,0:T(8,128)(2,1)S(1)}, bf16[2,128,1024]{2,1,0:T(8,128)(2,1)}, u32[]{:S(2)}) copy-start(bf16[2,128,1024]{2,1,0:T(8,128)(2,1)} %param.17) | copy-start | bytes 1572868
  879.3 65.2 %copy-start.53 = (f32[1024]{0:T(1024)S(1)}, f32[1024]{0:T(1024)}, u32[]{:S(2)}) copy-start(f32[1024]{0:T(1024)} %copy-done.52) | copy-start | bytes 12292
  879.4 65.2 %copy-start.64 = (f32[2,128]{1,0:T(2,128)S(1)}, f32[2,128]{1,0:T(2,128)}, u32[]{:S(2)}) copy-start(f32[2,128]{1,0:T(2,128)} %copy-done.63) | copy-start | bytes 3076
  879.4 65.2 %copy-start.90 = (f32[2,128]{1,0:T(2,128)S(1)}, f32[2,128]{1,0:T(2,128)}, u32[]{:S(2)}) copy-start(f32[2,128]{1,0:T(2,128)} %copy-done.89) | copy-start | bytes 3076
  879.4 456.1 %reduce-scatter.37.cloned.1.call-start = ((), (), s32[]{:S(2)}) async-start(), calls=%async_computation.36 | async-start | bytes 540672
  950.3 519.7 %reduce-scatter.39.cloned.1.call-start = ((), (), s32[]{:S(2)}) async-start(), calls=%async_computation.37 | async-start | bytes 540672
  954.6 553.0 %reduce-scatter.23.cloned.1.call-start = ((), (), s32[]{:S(2)}) async-start(), calls=%async_computation.23 | async-start | bytes 1769472 | tf_op jit(solution)/shard_map/reduce_scatter | solution.py:336
  956.7 592.4 %reduce-scatter.21.cloned.1.call-start = ((), (), s32[]{:S(2)}) async-start(), calls=%async_computation.22 | async-start | bytes 1769472 | tf_op jit(solution)/shard_map/reduce_scatter | solution.py:336
  958.7 240.1 %copy-start.33 = (f32[2,128,1024]{2,1,0:T(8,128)S(1)}, f32[2,128,1024]{2,1,0:T(8,128)}, u32[]{:S(2)}) copy-start(f32[2,128,1024]{2,1,0:T(8,128)} %get-tuple-element.616) | copy-start | bytes 3145732
  958.7 240.1 %copy-start.83 = (f32[1024]{0:T(1024)S(1)}, f32[1024]{0:T(1024)}, u32[]{:S(2)}) copy-start(f32[1024]{0:T(1024)} %get-tuple-element.604) | copy-start | bytes 12292
  (68 other events, 156.5 us)
Sparse Core Ops, SparseCore 0:
  10.5 28.6 all-gather.20
  203.9 14.2 all-gather.16
  231.1 50.0 all-reduce.8
  283.6 27.0 all-gather.22
  312.9 27.7 all-gather.24
  344.3 51.8 all-reduce.10
  398.1 24.8 all-gather.26
  425.9 16.6 all-gather.18
  451.9 51.8 all-reduce.12
  505.6 27.0 all-gather.28
  535.2 27.7 all-gather.30
  569.6 51.8 all-reduce.14
  649.3 30.4 reduce-scatter.16
  684.7 51.8 all-reduce.16
  745.5 51.1 all-reduce.18
  822.9 30.4 reduce-scatter.18
  858.3 86.1 all-reduce.20
  948.0 33.1 reduce-scatter.26
  984.9 34.0 reduce-scatter.24
  1022.1 41.0 reduce-scatter.30
  1066.5 41.1 reduce-scatter.28
  1111.0 41.1 reduce-scatter.34
  1155.4 41.1 reduce-scatter.32
  1199.3 136.1 reduce-scatter.36
  1337.7 132.2 reduce-scatter.38
  1473.1 34.3 reduce-scatter.22
  1510.7 38.3 reduce-scatter.20
where the time goes:
time: 1570 us; the launch traced here: 1560 us
  waiting for transfers between devices  1140 us (73%)
  blocking collectives  166 us (11%)
  other arithmetic  96.3 us (6%)
  matrix products  78.5 us (5%)
  local copies, waits for them, and re-layouts  57.6 us (4%)
  between operations  16.5 us (1%)
    unnamed x29, waiting for transfers between devices  270 us
    psum x2, waiting for transfers between devices, forward_layer(): result = mid + lax.psum(down, 'mp') + vec[5]  114 us
    psum x2, waiting for transfers between devices, per_device(): lax.psum(jnp.einsum('cju,xu->cjx', up_gradient_half_precision, up_weight,...  100 us
    psum x2, waiting for transfers between devices, forward_layer(): mid = state + lax.psum(part, 'mp') + vec[4]  95.2 us
    reduce_scatter x2, waiting for transfers between devices, per_device(): lax.psum_scatter(up_weight_gradient.astype(jnp.bfloat16), ('batch', 'ctx'...  87.1 us
    reduce_scatter x2, waiting for transfers between devices, per_device(): lax.psum_scatter(grad_wd.astype(jnp.bfloat16), ('batch', 'ctx'), scatter_...  86.8 us
    reduce_scatter x2, waiting for transfers between devices, per_device(): lax.psum_scatter(query_weight_gradient.astype(jnp.bfloat16), ('batch', 'c...  77.6 us
    all_gather x1, blocking collectives, per_device(): lax.all_gather(biases, ('batch', 'ctx', 'mp'), axis=2, tiled=True)  74.2 us
  transfers between devices with their start and end apart: 27, of which 25 were waited for; matrix products, arithmetic and copies ran while one was open for 8% of the time, Pallas kernels for 0%

commit v1 on v0

--- a/solution.py
+++ b/solution.py
@@ -198,7 +198,7 @@
         act, _ = gelu_parts(up_projected)
         act_bf = act.astype(jnp.bfloat16)
         down = jnp.einsum("slf,of->slo", act_bf, w_d, preferred_element_type=jnp.float32)
-        result = mid + lax.psum(down, "mp") + vec[5]
+        result = mid + jnp.sum(lax.all_gather(down, "mp"), axis=0) + vec[5]
         return (
             result,
             (

time: 1570 us -> 1640 us (1.045)
  waiting for transfers between devices: 1140 us -> 1220 us
    all_gather x0 -> x2, waiting for transfers between devices: none -> 159 us  [forward_layer(): result = mid + jnp.sum(lax.all_gather(down, 'mp'), axis=0) + vec[5]]
    psum x2 -> x0, waiting for transfers between devices: 114 us -> none  [forward_layer(): result = mid + lax.psum(down, 'mp') + vec[5]]
    psum x1 -> x2, waiting for transfers between devices: 52 us -> 83.4 us  [per_device(): lax.psum(jnp.einsum('aewu,vwu->aev', packed_projection_gradient, query_we...]
    unnamed x29 -> x30, waiting for transfers between devices: 270 us -> 271 us
  transfers between devices with their start and end apart: 27 -> 28, of which waited for: 25 -> 26; matrix products, arithmetic and copies ran while one was open for 8% -> 7% of each run, Pallas kernels for 0% -> 0%
where the time goes in v1:
time: 1640 us
  waiting for transfers between devices  1220 us (74%)
  blocking collectives  167 us (10%)
  other arithmetic  98 us (6%)
  matrix products  75.1 us (5%)
  local copies, waits for them, and re-layouts  57.1 us (3%)
  between operations  16.7 us (1%)
    unnamed x30, waiting for transfers between devices  271 us
    all_gather x2, waiting for transfers between devices, forward_layer(): result = mid + jnp.sum(lax.all_gather(down, 'mp'), axis=0) + vec[5]  159 us
    psum x2, waiting for transfers between devices, per_device(): lax.psum(jnp.einsum('cju,xu->cjx', up_gradient_half_precision, up_weight,...  96.4 us
    psum x2, waiting for transfers between devices, forward_layer(): mid = state + lax.psum(part, 'mp') + vec[4]  95.4 us
    reduce_scatter x2, waiting for transfers between devices, per_device(): lax.psum_scatter(up_weight_gradient.astype(jnp.bfloat16), ('batch', 'ctx'...  87.3 us
    reduce_scatter x2, waiting for transfers between devices, per_device(): lax.psum_scatter(grad_wd.astype(jnp.bfloat16), ('batch', 'ctx'), scatter_...  86.7 us
    psum x2, waiting for transfers between devices, per_device(): lax.psum(jnp.einsum('aewu,vwu->aev', packed_projection_gradient, query_we...  83.4 us
    reduce_scatter x2, waiting for transfers between devices, per_device(): lax.psum_scatter(query_weight_gradient.astype(jnp.bfloat16), ('batch', 'c...  78.3 us
  transfers between devices with their start and end apart: 28, of which 26 were waited for; matrix products, arithmetic and copies ran while one was open for 7% of the time, Pallas kernels for 0%

profile of v1, /device:TPU:0, one launch (start us, length us, event | category | flops | bytes accessed | tf_op | source)
XLA Modules:
  0.0 1636.5 jit_solution(6709615223059466036)
XLA Ops:
  10.7 74.2 %all_gather.63 = bf16[2,10,1024]{1,0,2:T(2,128)(2,1)S(1)} all-gather(bf16[2,10,32]{1,0,2:T(2,128)(2,1)S(1)} %copy.109), channel_id=1, replica_groups=mesh['batch'=2,'ctx'=4,'mp'=4] {'batch','ctx','mp'}, dimensions={2}, use_global_device_ids=true | all-gather | bytes 42240 | tf_op jit(solution)/shard_map/all_gather | solution.py:153
  84.8 2.5 fusion.155
  91.6 68.2 %all_gather.62 = bf16[2,2,1024]{1,0,2:T(2,128)(2,1)S(1)} all-gather(bf16[2,2,32]{1,0,2:T(2,128)(2,1)S(1)} %copy.108), channel_id=1, replica_groups=mesh['batch'=2,'ctx'=4,'mp'=4] {'batch','ctx','mp'}, dimensions={2}, use_global_device_ids=true | all-gather | bytes 8448 | tf_op jit(solution)/shard_map/all_gather | solution.py:152
  160.3 18.1 %fusion.103 = (f32[1024]{0:T(1024)S(1)}, f32[1024]{0:T(1024)S(1)}, f32[1024]{0:T(1024)S(1)}, f32[1024]{0:T(1024)S(1)}) fusion(bf16[2,2,1024]{1,0,2:T(2,128)(2,1)S(1)} %all_gather.62), kind=kLoop, calls=%fused_computation.161 | loop fusion | flops 4096 | bytes 24576 | tf_op jit(solution)/shard_map/mul | solution.py:191
  178.4 24.6 %fusion.101 = (f32[1024]{0:T(1024)S(1)}, f32[1024]{0:T(1024)S(1)}, f32[1024]{0:T(1024)S(1)}, f32[1024]{0:T(1024)}, f32[1024]{0:T(1024)S(1)}, /*index=5*/f32[1024]{0:T(1024)S(1)}, f32[1024]{0:T(1024)S(1)}, f32[1024]{0:T(1024)S(1)}) fusion(bf16[2,10,1024]{1,0,2:T(2,128)(2,1)S(1)} %all_gather.63), kind=kLoop, calls=%fused_computation.157 | loop fusion | flops 8192 | bytes 49152 | tf_op jit(solution)/shard_map/add | solution.py:201
  206.0 5.1 all_gather.61
  213.4 9.6 all-gather.1
  223.9 5.6 conditional.4
  226.4 2.5 fusion.148
  235.5 46.0 %all-reduce.7.cloned.1.call-done = f32[2,128,1024]{2,1,0:T(8,128)} async-done(((f32[2,128,1024]{2,1,0:T(8,128)}), f32[2,128,1024]{2,1,0:T(8,128)}) %all-reduce.7.cloned.1.call-update) | async-done | bytes 1048592 | tf_op jit(solution)/shard_map/psum | solution.py:189
  283.2 27.7 %all-gather.27.cloned.1.call-done = bf16[1,1024,1024]{2,1,0:T(8,128)(2,1)} async-done(((bf16[1,128,1024]{2,1,0:T(8,128)(2,1)}), bf16[1,1024,1024]{2,1,0:T(8,128)(2,1)}) %all-gather.27.cloned.1.call-update) | async-done | bytes 2097168 | tf_op jit(solution)/shard_map/all_gather | solution.py:224
  310.9 2.4 fusion.47
  313.3 27.7 %all-gather.29.cloned.1.call-done = bf16[1,1024,1024]{2,1,0:T(8,128)(2,1)} async-done(((bf16[1,128,1024]{2,1,0:T(8,128)(2,1)}), bf16[1,1024,1024]{2,1,0:T(8,128)(2,1)}) %all-gather.29.cloned.1.call-update) | async-done | bytes 2097168 | tf_op jit(solution)/shard_map/all_gather | solution.py:225
  341.0 3.4 fusion.26
  345.2 80.1 %all-gather.31.cloned.1.call-done = f32[8,128,1024]{2,1,0:T(8,128)} async-done(((f32[2,128,1024]{2,1,0:T(8,128)}), f32[8,128,1024]{2,1,0:T(8,128)}) %all-gather.31.cloned.1.call-update) | async-done | bytes 4194320 | tf_op jit(solution)/shard_map/all_gather | solution.py:201
  425.3 2.7 reduce_sum.420
  428.5 22.8 %all-gather.33.cloned.1.call-done = bf16[1,1024,3,256]{3,1,2,0:T(8,128)(2,1)} async-done(((bf16[1,128,3,256]{3,1,2,0:T(8,128)(2,1)}), bf16[1,1024,3,256]{3,1,2,0:T(8,128)(2,1)}) %all-gather.33.cloned.1.call-update) | async-done | bytes 1572880 | tf_op jit(solution)/shard_map/all_gather | solution.py:222
  454.2 9.8 all-gather.6
  464.8 6.2 all-gather.23.cloned.1.call-done
  471.0 6.5 conditional.5
  474.5 2.5 fusion.149
  481.5 49.4 %all-reduce.9.cloned.1.call-done = f32[2,128,1024]{2,1,0:T(8,128)} async-done(((f32[2,128,1024]{2,1,0:T(8,128)}), f32[2,128,1024]{2,1,0:T(8,128)}) %all-reduce.9.cloned.1.call-update) | async-done | bytes 1048592 | tf_op jit(solution)/shard_map/psum | solution.py:189
  532.7 27.7 %all-gather.35.cloned.1.call-done = bf16[1,1024,1024]{2,1,0:T(8,128)(2,1)} async-done(((bf16[1,128,1024]{2,1,0:T(8,128)(2,1)}), bf16[1,1024,1024]{2,1,0:T(8,128)(2,1)}) %all-gather.35.cloned.1.call-update) | async-done | bytes 2097168 | tf_op jit(solution)/shard_map/all_gather | solution.py:224
  560.3 3.3 fusion.53
  563.7 26.4 %all-gather.37.cloned.1.call-done = bf16[1,1024,1024]{2,1,0:T(8,128)(2,1)} async-done(((bf16[1,128,1024]{2,1,0:T(8,128)(2,1)}), bf16[1,1024,1024]{2,1,0:T(8,128)(2,1)}) %all-gather.37.cloned.1.call-update) | async-done | bytes 2097168 | tf_op jit(solution)/shard_map/all_gather | solution.py:225
  590.0 3.9 fusion.158
  596.6 3.8 fusion.18
  602.8 45.7 %all-reduce.11.cloned.1.call-done = f32[2,128,1024]{2,1,0:T(8,128)} async-done(((f32[2,128,1024]{2,1,0:T(8,128)}), f32[2,128,1024]{2,1,0:T(8,128)}) %all-reduce.11.cloned.1.call-update) | async-done | bytes 1048592 | tf_op jit(solution)/shard_map/psum | solution.py:271
  648.6 2.3 multiply_reduce_fusion
  650.9 79.3 %all-gather.39.cloned.1.call-done = f32[8,128,1024]{2,1,0:T(8,128)} async-done(((f32[2,128,1024]{2,1,0:T(8,128)}), f32[8,128,1024]{2,1,0:T(8,128)}) %all-gather.39.cloned.1.call-update) | async-done | bytes 4194320 | tf_op jit(solution)/shard_map/all_gather | solution.py:201
  730.2 3.7 reduce_sum.425
  733.9 3.7 fusion.140
  742.1 16.3 conditional.6
  744.6 2.3 copy.119
  746.9 2.4 exponential_select_fusion.3
  754.7 3.1 pad_maximum_fusion.1
  758.4 3.0 copy.120
  761.4 29.8 %reduce-scatter.17.cloned.1.call-done = f32[2,128,2,256]{3,1,2,0:T(8,128)} async-done(((f32[2,512,2,256]{3,1,2,0:T(8,128)}), f32[2,128,2,256]{3,1,2,0:T(8,128)}) %reduce-scatter.17.cloned.1.call-update) | async-done | bytes 524304 | tf_op jit(solution)/shard_map/reduce_scatter | solution.py:296
  793.0 3.0 fusion.44
  796.0 52.0 %all-reduce.13.cloned.1.call-done = f32[2,128,1024]{2,1,0:T(8,128)} async-done(((f32[2,128,1024]{2,1,0:T(8,128)}), f32[2,128,1024]{2,1,0:T(8,128)}) %all-reduce.13.cloned.1.call-update) | async-done | bytes 1048592 | tf_op jit(solution)/shard_map/psum | solution.py:309
  848.0 2.5 multiply_reduce_fusion.1
  857.4 50.7 %all-reduce.15.cloned.1.call-done = f32[2,128,1024]{2,1,0:T(8,128)} async-done(((f32[2,128,1024]{2,1,0:T(8,128)}), f32[2,128,1024]{2,1,0:T(8,128)}) %all-reduce.15.cloned.1.call-update) | async-done | bytes 1048592 | tf_op jit(solution)/shard_map/psum | solution.py:271
  908.1 2.5 multiply_reduce_fusion.2
  916.2 15.3 conditional.7
  918.9 2.3 copy.123
  921.2 2.3 exponential_select_fusion.2
  928.3 3.1 pad_maximum_fusion
  931.5 3.0 copy.124
  934.5 30.5 %reduce-scatter.19.cloned.1.call-done = f32[2,128,2,256]{3,1,2,0:T(8,128)} async-done(((f32[2,512,2,256]{3,1,2,0:T(8,128)}), f32[2,128,2,256]{3,1,2,0:T(8,128)}) %reduce-scatter.19.cloned.1.call-update) | async-done | bytes 524304 | tf_op jit(solution)/shard_map/reduce_scatter | solution.py:296
  966.8 3.1 fusion.41
  970.0 2.4 fusion.60
  972.5 2.4 fusion.59
  975.0 3.3 bitcast_convert_fusion.2
  990.6 31.4 %all-reduce.17.cloned.1.call-done = f32[2,128,1024]{2,1,0:T(8,128)} async-done(((f32[2,128,1024]{2,1,0:T(8,128)}), f32[2,128,1024]{2,1,0:T(8,128)}) %all-reduce.17.cloned.1.call-update) | async-done | bytes 1048592 | tf_op jit(solution)/shard_map/psum | solution.py:309
  1032.6 26.5 %reduce-scatter.27.cloned.1.call-done = bf16[128,256]{1,0:T(8,128)(2,1)} async-done(((bf16[1024,256]{1,0:T(8,128)(2,1)}), bf16[128,256]{1,0:T(8,128)(2,1)}) %reduce-scatter.27.cloned.1.call-update) | async-done | bytes 65552 | tf_op jit(solution)/shard_map/reduce_scatter | solution.py:342
  1059.1 37.7 %reduce-scatter.25.cloned.1.call-done = bf16[128,256]{1,0:T(8,128)(2,1)} async-done(((bf16[1024,256]{1,0:T(8,128)(2,1)}), bf16[128,256]{1,0:T(8,128)(2,1)}) %reduce-scatter.25.cloned.1.call-update) | async-done | bytes 65552 | tf_op jit(solution)/shard_map/reduce_scatter | solution.py:342
  1098.3 42.9 %reduce-scatter.31.cloned.1.call-done = bf16[128,1024]{1,0:T(8,128)(2,1)} async-done(((bf16[1024,1024]{1,0:T(8,128)(2,1)}), bf16[128,1024]{1,0:T(8,128)(2,1)}) %reduce-scatter.31.cloned.1.call-update) | async-done | bytes 262160 | tf_op jit(solution)/shard_map/reduce_scatter | solution.py:345
  1141.2 44.4 %reduce-scatter.29.cloned.1.call-done = bf16[128,1024]{1,0:T(8,128)(2,1)} async-done(((bf16[1024,1024]{1,0:T(8,128)(2,1)}), bf16[128,1024]{1,0:T(8,128)(2,1)}) %reduce-scatter.29.cloned.1.call-update) | async-done | bytes 262160 | tf_op jit(solution)/shard_map/reduce_scatter | solution.py:345
  1187.7 42.4 %reduce-scatter.35.cloned.1.call-done = bf16[128,1024]{1,0:T(8,128)(2,1)} async-done(((bf16[1024,1024]{1,0:T(8,128)(2,1)}), bf16[128,1024]{1,0:T(8,128)(2,1)}) %reduce-scatter.35.cloned.1.call-update) | async-done | bytes 262160 | tf_op jit(solution)/shard_map/reduce_scatter | solution.py:351
  1230.0 44.3 %reduce-scatter.33.cloned.1.call-done = bf16[128,1024]{1,0:T(8,128)(2,1)} async-done(((bf16[1024,1024]{1,0:T(8,128)(2,1)}), bf16[128,1024]{1,0:T(8,128)(2,1)}) %reduce-scatter.33.cloned.1.call-update) | async-done | bytes 262160 | tf_op jit(solution)/shard_map/reduce_scatter | solution.py:351
  1277.6 135.4 %reduce-scatter.37.cloned.1.call-done = f32[32,4]{1,0:T(8,128)} async-done(((f32[1024,4]{1,0:T(8,128)}), f32[32,4]{1,0:T(8,128)}) %reduce-scatter.37.cloned.1.call-update) | async-done | bytes 528
  1414.5 133.1 %reduce-scatter.39.cloned.1.call-done = f32[32,20]{1,0:T(8,128)} async-done(((f32[1024,20]{1,0:T(8,128)}), f32[32,20]{1,0:T(8,128)}) %reduce-scatter.39.cloned.1.call-update) | async-done | bytes 2576
  1549.1 36.7 %reduce-scatter.23.cloned.1.call-done = bf16[128,3,256]{2,0,1:T(8,128)(2,1)} async-done(((bf16[1024,3,256]{2,0,1:T(8,128)(2,1)}), bf16[128,3,256]{2,0,1:T(8,128)(2,1)}) %reduce-scatter.23.cloned.1.call-update) | async-done | bytes 196624 | tf_op jit(solution)/shard_map/reduce_scatter | solution.py:336
  1585.8 41.6 %reduce-scatter.21.cloned.1.call-done = bf16[128,3,256]{2,0,1:T(8,128)(2,1)} async-done(((bf16[1024,3,256]{2,0,1:T(8,128)(2,1)}), bf16[128,3,256]{2,0,1:T(8,128)(2,1)}) %reduce-scatter.21.cloned.1.call-update) | async-done | bytes 196624 | tf_op jit(solution)/shard_map/reduce_scatter | solution.py:336
  (419 shorter events, 114.8 us)
Async XLA Ops:
  7.2 195.9 %all-gather.25.cloned.1.call-start = ((), (), s32[]{:S(2)}) async-start(), calls=%async_computation.30 | async-start | bytes 1769472 | tf_op jit(solution)/shard_map/all_gather | solution.py:222
  9.0 214.8 %all-gather.21.cloned.1.call-start = ((), (), s32[]{:S(2)}) async-start(), calls=%async_computation.12 | async-start | bytes 1310720 | tf_op jit(solution)/shard_map/all_gather | solution.py:184
  84.8 74.9 %copy-start.4 = (bf16[2,128,1024]{2,1,0:T(8,128)(2,1)S(1)}, bf16[2,128,1024]{2,1,0:T(8,128)(2,1)}, u32[]{:S(2)}) copy-start(bf16[2,128,1024]{2,1,0:T(8,128)(2,1)} %param.17) | copy-start | bytes 1572868
  159.9 43.1 %copy-start.61 = (f32[2,128]{1,0:T(2,128)}, f32[2,128]{1,0:T(2,128)S(1)}, u32[]{:S(2)}) copy-start(f32[2,128]{1,0:T(2,128)S(1)} %broadcast_multiply_fusion.15) | copy-start | bytes 3076
  160.2 42.9 %copy-start.86 = (f32[2,128]{1,0:T(2,128)}, f32[2,128]{1,0:T(2,128)S(1)}, u32[]{:S(2)}) copy-start(f32[2,128]{1,0:T(2,128)S(1)} %add_rsqrt_fusion.3) | copy-start | bytes 3076
  178.4 24.6 %copy-start.50 = (f32[1024]{0:T(1024)}, f32[1024]{0:T(1024)S(1)}, u32[]{:S(2)}) copy-start(f32[1024]{0:T(1024)S(1)} %get-tuple-element.615) | copy-start | bytes 12292
  178.4 272.9 %copy-start.52 = (f32[1024]{0:T(1024)}, f32[1024]{0:T(1024)S(1)}, u32[]{:S(2)}) copy-start(f32[1024]{0:T(1024)S(1)} %get-tuple-element.613) | copy-start | bytes 12292
  203.0 107.8 %copy-start.79 = (f32[1024]{0:T(1024)}, f32[1024]{0:T(1024)S(1)}, u32[]{:S(2)}) copy-start(f32[1024]{0:T(1024)S(1)} %get-tuple-element.609) | copy-start | bytes 12292
  203.0 357.3 %copy-start.81 = (f32[1024]{0:T(1024)}, f32[1024]{0:T(1024)S(1)}, u32[]{:S(2)}) copy-start(f32[1024]{0:T(1024)S(1)} %get-tuple-element.605) | copy-start | bytes 12292
  203.1 10.3 copy-start.49
  205.9 75.5 %all-reduce.7.cloned.1.call-start = ((), (), s32[]{:S(2)}) async-start(), calls=%async_computation.13 | async-start | bytes 2097152 | tf_op jit(solution)/shard_map/psum | solution.py:189
  211.1 259.9 %copy-start.85 = (s32[128]{0:T(128)}, s32[128]{0:T(128)S(1)}, u32[]{:S(2)}) copy-start(s32[128]{0:T(128)S(1)} %iota_add_fusion) | copy-start | bytes 1540
  213.4 257.6 %copy-start.91 = (f32[4]{0:T(128)}, f32[4]{0:T(128)S(1)}, u32[]{:S(2)}) copy-start(f32[4]{0:T(128)S(1)} %multiply_exponential_fusion) | copy-start | bytes 52
  223.0 6.5 copy-start.9
  230.9 80.0 %all-gather.27.cloned.1.call-start = ((), (), s32[]{:S(2)}) async-start(), calls=%async_computation.31 | async-start | bytes 2359296 | tf_op jit(solution)/shard_map/all_gather | solution.py:224
  231.8 109.2 %all-gather.29.cloned.1.call-start = ((), (), s32[]{:S(2)}) async-start(), calls=%async_computation.32 | async-start | bytes 2359296 | tf_op jit(solution)/shard_map/all_gather | solution.py:225
  232.7 192.6 %all-gather.31.cloned.1.call-start = ((), (), s32[]{:S(2)}) async-start(), calls=%async_computation.33 | async-start | bytes 5242880 | tf_op jit(solution)/shard_map/all_gather | solution.py:201
  282.9 30.3 %copy-start.54 = (f32[2,128]{1,0:T(2,128)}, f32[2,128]{1,0:T(2,128)S(1)}, u32[]{:S(2)}) copy-start(f32[2,128]{1,0:T(2,128)S(1)} %broadcast_multiply_fusion.14) | copy-start | bytes 3076
  283.2 30.1 %copy-start.63 = (f32[2,128]{1,0:T(2,128)}, f32[2,128]{1,0:T(2,128)S(1)}, u32[]{:S(2)}) copy-start(f32[2,128]{1,0:T(2,128)S(1)} %add_rsqrt_fusion.2) | copy-start | bytes 3076
  313.3 31.1 %copy-start.38 = (f32[2,128,1024]{2,1,0:T(8,128)}, f32[2,128,1024]{2,1,0:T(8,128)S(1)}, u32[]{:S(2)}) copy-start(f32[2,128,1024]{2,1,0:T(8,128)S(1)} %fusion.47) | copy-start | bytes 3145732
  344.4 106.9 %all-gather.33.cloned.1.call-start = ((), (), s32[]{:S(2)}) async-start(), calls=%async_computation.34 | async-start | bytes 1769472 | tf_op jit(solution)/shard_map/all_gather | solution.py:222
  345.2 125.8 %all-gather.23.cloned.1.call-start = ((), (), s32[]{:S(2)}) async-start(), calls=%async_computation.14 | async-start | bytes 1310720 | tf_op jit(solution)/shard_map/all_gather | solution.py:184
  428.0 23.3 %copy-start.100 = (f32[1024]{0:T(1024)S(1)}, f32[1024]{0:T(1024)}, u32[]{:S(2)}) copy-start(f32[1024]{0:T(1024)} %get-tuple-element.607) | copy-start | bytes 12292
  428.2 25.1 %copy-start.76 = (f32[2,128]{1,0:T(2,128)}, f32[2,128]{1,0:T(2,128)S(1)}, u32[]{:S(2)}) copy-start(f32[2,128]{1,0:T(2,128)S(1)} %broadcast_multiply_fusion.13) | copy-start | bytes 3076
  428.5 25.6 %copy-start.88 = (f32[2,128]{1,0:T(2,128)}, f32[2,128]{1,0:T(2,128)S(1)}, u32[]{:S(2)}) copy-start(f32[2,128]{1,0:T(2,128)S(1)} %add_rsqrt_fusion.1) | copy-start | bytes 3076
  454.1 76.8 %all-reduce.9.cloned.1.call-start = ((), (), s32[]{:S(2)}) async-start(), calls=%async_computation.15 | async-start | bytes 2097152 | tf_op jit(solution)/shard_map/psum | solution.py:189
  464.0 13.6 copy-start.11
  477.5 53.4 %copy-start.32 = (bf16[2,128,4,64]{1,3,2,0:T(8,128)(2,1)}, bf16[2,128,4,64]{1,3,2,0:T(8,128)(2,1)S(1)}, u32[]{:S(2)}) copy-start(bf16[2,128,4,64]{1,3,2,0:T(8,128)(2,1)S(1)} %divide_convert_fusion) | copy-start | bytes 393220
  478.9 81.4 %all-gather.35.cloned.1.call-start = ((), (), s32[]{:S(2)}) async-start(), calls=%async_computation.35 | async-start | bytes 2359296 | tf_op jit(solution)/shard_map/all_gather | solution.py:224
  479.5 110.6 %all-gather.37.cloned.1.call-start = ((), (), s32[]{:S(2)}) async-start(), calls=%async_computation.36 | async-start | bytes 2359296 | tf_op jit(solution)/shard_map/all_gather | solution.py:225
  480.2 168.3 %all-reduce.11.cloned.1.call-start = ((), (), s32[]{:S(2)}) async-start(), calls=%async_computation.16 | async-start | bytes 2097152 | tf_op jit(solution)/shard_map/psum | solution.py:271
  532.4 201.5 %copy-start.57 = (f32[2,128]{1,0:T(2,128)}, f32[2,128]{1,0:T(2,128)S(1)}, u32[]{:S(2)}) copy-start(f32[2,128]{1,0:T(2,128)S(1)} %broadcast_multiply_fusion.12) | copy-start | bytes 3076
  532.6 201.2 %copy-start.66 = (f32[2,128]{1,0:T(2,128)}, f32[2,128]{1,0:T(2,128)S(1)}, u32[]{:S(2)}) copy-start(f32[2,128]{1,0:T(2,128)S(1)} %add_rsqrt_fusion) | copy-start | bytes 3076
  596.5 133.7 %all-gather.39.cloned.1.call-start = ((), (), s32[]{:S(2)}) async-start(), calls=%async_computation.37 | async-start | bytes 5242880 | tf_op jit(solution)/shard_map/all_gather | solution.py:201
  600.4 190.8 %reduce-scatter.17.cloned.1.call-start = ((), (), s32[]{:S(2)}) async-start(), calls=%async_computation.17 | async-start | bytes 2621440 | tf_op jit(solution)/shard_map/reduce_scatter | solution.py:296
  758.4 33.9 %copy-start.43 = (bf16[2,128,1,256]{3,1,2,0:T(8,128)(2,1)}, bf16[2,128,1,256]{3,1,2,0:T(8,128)(2,1)S(1)}, u32[]{:S(2)}) copy-start(bf16[2,128,1,256]{3,1,2,0:T(8,128)(2,1)S(1)} %get-tuple-element.586) | copy-start | bytes 393220
  761.4 86.7 %all-reduce.13.cloned.1.call-start = ((), (), s32[]{:S(2)}) async-start(), calls=%async_computation.18 | async-start | bytes 2097152 | tf_op jit(solution)/shard_map/psum | solution.py:309
  792.3 55.8 %copy-start.53 = (f32[1024]{0:T(1024)S(1)}, f32[1024]{0:T(1024)}, u32[]{:S(2)}) copy-start(f32[1024]{0:T(1024)} %copy-done.52) | copy-start | bytes 12292
  796.0 54.6 %copy-start.77 = (f32[2,128]{1,0:T(2,128)S(1)}, f32[2,128]{1,0:T(2,128)}, u32[]{:S(2)}) copy-start(f32[2,128]{1,0:T(2,128)} %copy-done.76) | copy-start | bytes 3076
  796.0 54.6 %copy-start.89 = (f32[2,128]{1,0:T(2,128)S(1)}, f32[2,128]{1,0:T(2,128)}, u32[]{:S(2)}) copy-start(f32[2,128]{1,0:T(2,128)} %copy-done.88) | copy-start | bytes 3076
  796.0 112.1 %all-reduce.15.cloned.1.call-start = ((), (), s32[]{:S(2)}) async-start(), calls=%async_computation.19 | async-start | bytes 2097152 | tf_op jit(solution)/shard_map/psum | solution.py:271
  855.1 53.1 %copy-start.55 = (f32[2,128]{1,0:T(2,128)S(1)}, f32[2,128]{1,0:T(2,128)}, u32[]{:S(2)}) copy-start(f32[2,128]{1,0:T(2,128)} %copy-done.54) | copy-start | bytes 3076
  855.1 53.1 %copy-start.64 = (f32[2,128]{1,0:T(2,128)S(1)}, f32[2,128]{1,0:T(2,128)}, u32[]{:S(2)}) copy-start(f32[2,128]{1,0:T(2,128)} %copy-done.63) | copy-start | bytes 3076
  856.8 108.3 %reduce-scatter.19.cloned.1.call-start = ((), (), s32[]{:S(2)}) async-start(), calls=%async_computation.20 | async-start | bytes 2621440 | tf_op jit(solution)/shard_map/reduce_scatter | solution.py:296
  931.5 34.7 %copy-start.45 = (bf16[2,128,1,256]{3,1,2,0:T(8,128)(2,1)}, bf16[2,128,1,256]{3,1,2,0:T(8,128)(2,1)S(1)}, u32[]{:S(2)}) copy-start(bf16[2,128,1,256]{3,1,2,0:T(8,128)(2,1)S(1)} %get-tuple-element.587) | copy-start | bytes 393220
  934.5 87.5 %all-reduce.17.cloned.1.call-start = ((), (), s32[]{:S(2)}) async-start(), calls=%async_computation.21 | async-start | bytes 2097152 | tf_op jit(solution)/shard_map/psum | solution.py:309
  970.0 89.1 %reduce-scatter.27.cloned.1.call-start = ((), (), s32[]{:S(2)}) async-start(), calls=%async_computation.25 | async-start | bytes 589824 | tf_op jit(solution)/shard_map/reduce_scatter | solution.py:342
  972.4 124.3 %reduce-scatter.25.cloned.1.call-start = ((), (), s32[]{:S(2)}) async-start(), calls=%async_computation.24 | async-start | bytes 589824 | tf_op jit(solution)/shard_map/reduce_scatter | solution.py:342
  974.9 166.3 %reduce-scatter.31.cloned.1.call-start = ((), (), s32[]{:S(2)}) async-start(), calls=%async_computation.27 | async-start | bytes 2359296 | tf_op jit(solution)/shard_map/reduce_scatter | solution.py:345
  978.3 207.3 %reduce-scatter.29.cloned.1.call-start = ((), (), s32[]{:S(2)}) async-start(), calls=%async_computation.26 | async-start | bytes 2359296 | tf_op jit(solution)/shard_map/reduce_scatter | solution.py:345
  981.5 248.5 %reduce-scatter.35.cloned.1.call-start = ((), (), s32[]{:S(2)}) async-start(), calls=%async_computation.29 | async-start | bytes 2359296 | tf_op jit(solution)/shard_map/reduce_scatter | solution.py:351
  984.9 289.4 %reduce-scatter.33.cloned.1.call-start = ((), (), s32[]{:S(2)}) async-start(), calls=%async_computation.28 | async-start | bytes 2359296 | tf_op jit(solution)/shard_map/reduce_scatter | solution.py:351
  988.8 33.2 %copy-start.5 = (bf16[2,128,1024]{2,1,0:T(8,128)(2,1)S(1)}, bf16[2,128,1024]{2,1,0:T(8,128)(2,1)}, u32[]{:S(2)}) copy-start(bf16[2,128,1024]{2,1,0:T(8,128)(2,1)} %param.17) | copy-start | bytes 1572868
  988.8 33.2 %copy-start.51 = (f32[1024]{0:T(1024)S(1)}, f32[1024]{0:T(1024)}, u32[]{:S(2)}) copy-start(f32[1024]{0:T(1024)} %copy-done.50) | copy-start | bytes 12292
  988.8 33.2 %copy-start.62 = (f32[2,128]{1,0:T(2,128)S(1)}, f32[2,128]{1,0:T(2,128)}, u32[]{:S(2)}) copy-start(f32[2,128]{1,0:T(2,128)} %copy-done.61) | copy-start | bytes 3076
  988.8 33.2 %copy-start.87 = (f32[2,128]{1,0:T(2,128)S(1)}, f32[2,128]{1,0:T(2,128)}, u32[]{:S(2)}) copy-start(f32[2,128]{1,0:T(2,128)} %copy-done.86) | copy-start | bytes 3076
  988.8 34.9 %copy-start.72 = (f32[1024]{0:T(1024)S(1)}, f32[1024]{0:T(1024)}, u32[]{:S(2)}) copy-start(f32[1024]{0:T(1024)} %get-tuple-element.588) | copy-start | bytes 12292
  988.9 424.2 %reduce-scatter.37.cloned.1.call-start = ((), (), s32[]{:S(2)}) async-start(), calls=%async_computation.38 | async-start | bytes 540672
  990.6 35.2 %copy-start.70 = (f32[1024]{0:T(1024)S(1)}, f32[1024]{0:T(1024)}, u32[]{:S(2)}) copy-start(f32[1024]{0:T(1024)} %get-tuple-element.600) | copy-start | bytes 12292
  1025.9 521.7 %reduce-scatter.39.cloned.1.call-start = ((), (), s32[]{:S(2)}) async-start(), calls=%async_computation.39 | async-start | bytes 540672
  1028.2 557.6 %reduce-scatter.23.cloned.1.call-start = ((), (), s32[]{:S(2)}) async-start(), calls=%async_computation.23 | async-start | bytes 1769472 | tf_op jit(solution)/shard_map/reduce_scatter | solution.py:336
  1030.5 596.9 %reduce-scatter.21.cloned.1.call-start = ((), (), s32[]{:S(2)}) async-start(), calls=%async_computation.22 | async-start | bytes 1769472 | tf_op jit(solution)/shard_map/reduce_scatter | solution.py:336
  1032.6 243.9 %copy-start.1 = (f32[2,128,1024]{2,1,0:T(8,128)S(1)}, f32[2,128,1024]{2,1,0:T(8,128)}, u32[]{:S(2)}) copy-start(f32[2,128,1024]{2,1,0:T(8,128)} %copy-done) | copy-start | bytes 3145732
  1032.6 243.8 %copy-start.13 = (f32[2,128,1024]{2,1,0:T(8,128)S(1)}, f32[2,128,1024]{2,1,0:T(8,128)}, u32[]{:S(2)}) copy-start(f32[2,128,1024]{2,1,0:T(8,128)} %all-reduce.17.cloned.1.call-done) | copy-start | bytes 3145732
  (68 other events, 155.5 us)
Sparse Core Ops, SparseCore 0:
  10.5 28.6 all-gather.24
  206.1 14.9 all-gather.20
  231.0 50.4 all-reduce.6
  283.8 27.0 all-gather.26
  313.2 27.7 all-gather.28
  344.5 80.7 all-gather.30
  427.2 24.0 all-gather.32
  454.2 16.6 all-gather.22
  479.0 51.8 all-reduce.8
  533.3 27.0 all-gather.34
  562.2 27.7 all-gather.36
  596.6 51.8 all-reduce.10
  650.1 79.9 all-gather.38
  761.5 29.6 reduce-scatter.16
  796.1 51.8 all-reduce.12
  856.9 51.1 all-reduce.14
  934.6 30.4 reduce-scatter.18
  970.1 51.9 all-reduce.16
  1025.7 33.3 reduce-scatter.26
  1062.6 34.1 reduce-scatter.24
  1100.0 41.1 reduce-scatter.30
  1144.5 41.0 reduce-scatter.28
  1188.9 41.1 reduce-scatter.34
  1233.2 41.1 reduce-scatter.32
  1277.1 135.8 reduce-scatter.36
  1415.1 132.4 reduce-scatter.38
  1550.8 35.0 reduce-scatter.22
  1589.1 38.3 reduce-scatter.20
